TPU v7x, 256 devices: a whole 4x4x8 slice. The times are simulated.
256 devices in a mesh: gx: 32 (over y, z), gy: 8 (over x, core).
Axes of the slice: x: 4, y: 4, z: 8, core: 2. Of those that a mesh axis runs over, the one named last changes fastest.
Arguments:
- features: bfloat16 [2048, 64, 512], P(('gx', 'gy')), may hold values from -6 to 6
- neighbours: int32 [2048, 6], P(('gx', 'gy')), may hold values from 0 to 16, as said below
- counts: int32 [256], P(('gx', 'gy')), may hold values from 1 to 8, as said below
- conv_weight: bfloat16 [64, 448], replicated, may hold values from -0.25 to 0.25
- down_weight: bfloat16 [128, 512], replicated, may hold values from -0.25 to 0.25
- head_weight: bfloat16 [128, 128], replicated, may hold values from -0.5 to 0.5
- coarse_map: int32 [256, 8], P(('gx', 'gy')), may hold values from 0 to 32, as said below
- latent_grad: bfloat16 [256, 512, 128], P(('gx', 'gy')), may hold values from -6 to 6
Outputs:
- latent: bfloat16 [256, 512, 128], P(('gx', 'gy'))
- features_grad: bfloat16 [2048, 64, 512], P(('gx', 'gy'))
- conv_grad: float32 [64, 448], replicated
- down_grad: float32 [128, 512], replicated
- head_grad: float32 [128, 128], replicated
Inputs may be any that keep to these rules, and one draw needn't show every extreme that they name: `counts`: in every draw, max(1, (devices along gx times devices along gy) // 8) columns have exactly 8 active blocks; each other column has between 1 and 4. 16 means no neighbour; a value below 8 is an active slot of the same column; a value v of 8 or more is the active slot v - 8 of the adjacent column in that direction; the z directions never name another column; inactive slots have no neighbours. `coarse_map`: 32 marks an empty octant; every other entry names an active block's octant, and each such octant is named at most once among the four columns that share a merged list.
All inputs are finite; a program needn't handle non-finite values.
Results may differ from a plain program's by a relative error of at most 0.013.
Values may be sent and summed in bfloat16 or wider, within the bound.
A program may use at most 128 MiB of HBM per device.

v0:
```python
import jax
import jax.numpy as jnp
from jax import lax
from jax.sharding import PartitionSpec as P


def from_partner(block, axis, distance):
    count = lax.axis_size(axis)
    route = []
    for low in range(count):
        high = low | 1 << distance
        if high != low and high < count:
            route += [(low, high), (high, low)]
    return lax.ppermute(block, axis, route)


def padded(block, sides, width):
    for axis, dim in sides:
        count = lax.axis_size(axis)
        forward = [(i, i + 1) for i in range(count - 1)]
        backward = [(target, source) for source, target in forward]
        low = lax.ppermute(
            lax.slice_in_dim(block, block.shape[dim] - width, None, axis=dim), axis, forward
        )
        high = lax.ppermute(lax.slice_in_dim(block, 0, width, axis=dim), axis, backward)
        block = jnp.concatenate([low, block, high], axis=dim)
    return block


def silu_grad(values):
    sigmoid_value = jax.nn.sigmoid(values)
    return sigmoid_value * (1.0 + values * (1.0 - sigmoid_value))


def octet(volume):
    return volume.reshape(volume.shape[0], volume.shape[1], 2, 2, 2, 4, 4, 4)


def face_of(cube, axis_number, upper):
    number, channels = (cube.shape[0], cube.shape[1])
    plane = lax.index_in_dim(cube, 3 if upper else 0, 5 + axis_number, keepdims=False)
    plane = lax.index_in_dim(plane, 1 if upper else 0, 2 + axis_number, keepdims=False)
    return plane.reshape(number, channels * 64)


def face_index(axis_number, upper):
    index = [slice(None)] * 8
    index[2 + axis_number] = 1 if upper else 0
    index[5 + axis_number] = 3 if upper else 0
    return tuple(index)


def expand_plane(rows, cube, axis_number):
    number, channels = (cube.shape[0], cube.shape[1])
    return jnp.expand_dims(
        rows.reshape(number, channels, 2, 2, 4, 4), (2 + axis_number, 5 + axis_number)
    )


def shift_minus(cube, rows, axis_number):
    parity, place = (2 + axis_number, 5 + axis_number)
    plane = expand_plane(rows, cube, axis_number)
    lower = lax.slice_in_dim(cube, 0, 1, axis=parity)
    upper = lax.slice_in_dim(cube, 1, 2, axis=parity)
    out_low = jnp.concatenate([plane, lax.slice_in_dim(upper, 0, 3, axis=place)], axis=place)
    return jnp.concatenate([out_low, lower], axis=parity)


def shift_plus(cube, rows, axis_number):
    parity, place = (2 + axis_number, 5 + axis_number)
    plane = expand_plane(rows, cube, axis_number)
    lower = lax.slice_in_dim(cube, 0, 1, axis=parity)
    upper = lax.slice_in_dim(cube, 1, 2, axis=parity)
    out_high = jnp.concatenate([lax.slice_in_dim(lower, 1, 4, axis=place), plane], axis=place)
    return jnp.concatenate([upper, out_high], axis=parity)


def minus_back(grad_out, axis_number):
    parity, place = (2 + axis_number, 5 + axis_number)
    grad_low = lax.slice_in_dim(grad_out, 0, 1, axis=parity)
    grad_high = lax.slice_in_dim(grad_out, 1, 2, axis=parity)
    moved = jnp.concatenate(
        [
            lax.slice_in_dim(grad_low, 1, 4, axis=place),
            jnp.zeros_like(lax.slice_in_dim(grad_low, 0, 1, axis=place)),
        ],
        axis=place,
    )
    plane = lax.index_in_dim(
        lax.index_in_dim(grad_low, 0, place, keepdims=False), 0, parity, keepdims=False
    )
    return (jnp.concatenate([grad_high, moved], axis=parity), plane)


def plus_back(grad_out, axis_number):
    parity, place = (2 + axis_number, 5 + axis_number)
    grad_low = lax.slice_in_dim(grad_out, 0, 1, axis=parity)
    grad_high = lax.slice_in_dim(grad_out, 1, 2, axis=parity)
    moved = jnp.concatenate(
        [
            jnp.zeros_like(lax.slice_in_dim(grad_high, 0, 1, axis=place)),
            lax.slice_in_dim(grad_high, 0, 3, axis=place),
        ],
        axis=place,
    )
    plane = lax.index_in_dim(
        lax.index_in_dim(grad_high, 3, place, keepdims=False), 0, parity, keepdims=False
    )
    return (jnp.concatenate([moved, grad_low], axis=parity), plane)


def face_layers(cube):
    return (
        face_of(cube, 0, True),
        face_of(cube, 0, False),
        face_of(cube, 1, True),
        face_of(cube, 1, False),
        face_of(cube, 2, True),
        face_of(cube, 2, False),
    )


def pick_rows(local_rows, remote_rows, index):
    width = local_rows.shape[1]
    pooled = jnp.concatenate(
        [local_rows, remote_rows, jnp.zeros((1, width), local_rows.dtype)], axis=0
    )
    return pooled[index]


def neighbour_stack(cube, faces, remotes, links):
    number, channels = (cube.shape[0], cube.shape[1])
    blank = jnp.zeros_like(faces[4])
    sources = (remotes[0], remotes[1], remotes[2], remotes[3], blank, blank)
    picked = [
        pick_rows(faces[direction], sources[direction], links[:, direction])
        for direction in range(6)
    ]
    fields = [
        cube,
        shift_minus(cube, picked[0], 0),
        shift_plus(cube, picked[1], 0),
        shift_minus(cube, picked[2], 1),
        shift_plus(cube, picked[3], 1),
        shift_minus(cube, picked[4], 2),
        shift_plus(cube, picked[5], 2),
    ]
    return jnp.stack(fields, axis=1).reshape(number, 7 * channels, 512)


def stack_grad(taps_grad, links):
    number, channels = (taps_grad.shape[0], taps_grad.shape[1] // 7)
    parts = taps_grad.reshape(number, 7, channels, 2, 2, 2, 4, 4, 4)
    grad_cube = parts[:, 0]
    face_grads = []
    for direction in range(6):
        axis_number = direction // 2
        if direction % 2 == 0:
            moved, plane = minus_back(parts[:, direction + 1], axis_number)
        else:
            moved, plane = plus_back(parts[:, direction + 1], axis_number)
        grad_cube = grad_cube + moved
        face_grads.append(plane.reshape(number, channels * 64))
    pools = [
        jnp.zeros((2 * number + 1, channels * 64), jnp.float32)
        .at[links[:, direction]]
        .add(face_grads[direction])
        for direction in range(6)
    ]
    for direction in range(6):
        shaped = pools[direction][:number].reshape(number, channels, 2, 2, 4, 4)
        grad_cube = grad_cube.at[face_index(direction // 2, direction % 2 == 0)].add(shaped)
    far_rows = [
        pools[direction][number : 2 * number].astype(jnp.bfloat16) for direction in range(4)
    ]
    return (grad_cube, far_rows)


def add_faces(grad_cube, into_xhigh, into_xlow, into_yhigh, into_ylow):
    number, channels = (grad_cube.shape[0], grad_cube.shape[1])

    def planes(rows):
        return rows.astype(jnp.float32).reshape(number, channels, 2, 2, 4, 4)

    grad_cube = grad_cube.at[face_index(0, True)].add(planes(into_xhigh))
    grad_cube = grad_cube.at[face_index(0, False)].add(planes(into_xlow))
    grad_cube = grad_cube.at[face_index(1, True)].add(planes(into_yhigh))
    grad_cube = grad_cube.at[face_index(1, False)].add(planes(into_ylow))
    return grad_cube


def merge_pool(own_rows):
    beside_y = from_partner(own_rows, "gy", 0)
    received = from_partner(jnp.concatenate([own_rows, beside_y], axis=0), "gx", 0)
    half = own_rows.shape[0]
    return jnp.concatenate([own_rows, received[:half], beside_y, received[half:]], axis=0)


def split_pool(back_rows):
    half = back_rows.shape[0] // 4
    own_part = back_rows[:half].astype(jnp.float32)
    along_x = back_rows[half : 2 * half]
    along_y = back_rows[2 * half : 3 * half]
    diagonal = back_rows[3 * half :]
    returned = from_partner(jnp.concatenate([along_x, diagonal], axis=0), "gx", 0)
    kept = own_part + returned[:half].astype(jnp.float32)
    beside = (along_y.astype(jnp.float32) + returned[half:].astype(jnp.float32)).astype(
        jnp.bfloat16
    )
    final_rows = kept + from_partner(beside, "gy", 0).astype(jnp.float32)
    return final_rows.astype(jnp.bfloat16)


def scatter_rows(volume, links, number):
    width = volume.shape[1] * volume.shape[2] // 8
    rows = volume.reshape(volume.shape[0] * 8, width)
    total = (
        jnp.zeros((4 * number + 1, width), jnp.float32)
        .at[links.reshape(-1)]
        .add(rows.astype(jnp.float32))
    )
    return total[: 4 * number].astype(jnp.bfloat16)


def body(
    features, neighbours, counts, conv_weight, down_weight, head_weight, coarse_map, latent_grad
):
    number, channels = (features.shape[0], features.shape[1])
    wide = down_weight.shape[0]
    coarse_count = coarse_map.shape[0]
    active = jnp.arange(number) < counts[0]
    masked = jnp.where(active[:, None, None], features, jnp.zeros((), jnp.bfloat16))
    cube = octet(masked)
    faces = face_layers(cube)
    rim_x = padded(jnp.stack([faces[1], faces[0]]), (("gx", 0),), 1)
    rim_y = padded(jnp.stack([faces[3], faces[2]]), (("gy", 0),), 1)
    taps = neighbour_stack(cube, faces, (rim_x[0], rim_x[3], rim_y[0], rim_y[3]), neighbours)
    hidden = jnp.einsum("ok,bkv->bov", conv_weight, taps, preferred_element_type=jnp.float32)
    act = jax.nn.silu(hidden).astype(jnp.bfloat16)
    patches = act.reshape(number, channels * 8, 64)
    octants = jnp.einsum(
        "ok,bkv->bvo", down_weight, patches, preferred_element_type=jnp.float32
    ).astype(jnp.bfloat16)
    empty_row = jnp.zeros((1, 64 * wide), jnp.bfloat16)
    merged = merge_pool(octants.reshape(number, 64 * wide))
    coarse = jnp.concatenate([merged, empty_row], axis=0)[coarse_map].reshape(
        coarse_count, 512, wide
    )
    coarse_act = jax.nn.silu(coarse.astype(jnp.float32)).astype(jnp.bfloat16)
    latent = jnp.einsum(
        "oi,cvi->cvo", head_weight, coarse_act, preferred_element_type=jnp.float32
    ).astype(jnp.bfloat16)
    act_grad = jnp.einsum(
        "oi,cvo->cvi", head_weight, latent_grad, preferred_element_type=jnp.float32
    )
    coarse_grad = (act_grad * silu_grad(coarse.astype(jnp.float32))).astype(jnp.bfloat16)
    head_part = jnp.einsum(
        "cvo,cvi->oi", latent_grad, coarse_act, preferred_element_type=jnp.float32
    )
    octant_grad = split_pool(scatter_rows(coarse_grad, coarse_map, number)).reshape(
        number, 64, wide
    )
    down_part = jnp.einsum("bvo,bkv->ok", octant_grad, patches, preferred_element_type=jnp.float32)
    patch_grad = jnp.einsum(
        "ok,bvo->bkv", down_weight, octant_grad, preferred_element_type=jnp.float32
    )
    hidden_grad = (patch_grad.reshape(number, channels, 512) * silu_grad(hidden)).astype(
        jnp.bfloat16
    )
    conv_part = jnp.einsum("bov,bkv->ok", hidden_grad, taps, preferred_element_type=jnp.float32)
    taps_grad = jnp.einsum(
        "ok,bov->bkv", conv_weight, hidden_grad, preferred_element_type=jnp.float32
    )
    near_grad, far_rows = stack_grad(taps_grad, neighbours)
    return_x = padded(jnp.stack([far_rows[0], far_rows[1]]), (("gx", 0),), 1)
    return_y = padded(jnp.stack([far_rows[2], far_rows[3]]), (("gy", 0),), 1)
    total_grad = add_faces(near_grad, return_x[3], return_x[0], return_y[3], return_y[0]).reshape(
        number, channels, 512
    )
    features_grad = jnp.where(active[:, None, None], total_grad, 0.0).astype(jnp.bfloat16)
    summed = lax.psum((conv_part, down_part, head_part), ("gx", "gy"))
    scale = float(number * lax.axis_size("gx") * lax.axis_size("gy")) ** (-0.5)
    return (latent, features_grad, summed[0] * scale, summed[1] * scale, summed[2] * scale)


def solution(mesh):
    placed = (
        P(("gx", "gy"), None, None),
        P(("gx", "gy"), None),
        P(("gx", "gy")),
        P(),
        P(),
        P(),
        P(("gx", "gy"), None),
        P(("gx", "gy"), None, None),
    )
    return jax.shard_map(
        body,
        mesh=mesh,
        in_specs=placed,
        out_specs=(P(("gx", "gy"), None, None), P(("gx", "gy"), None, None), P(), P(), P()),
        check_vma=False,
    )
```

profile of v0, /device:TPU:2, one launch (start us, length us, event | category | flops | bytes accessed | tf_op | source)
XLA Modules:
  0.0 611.6 jit_solution(5561831385059505792)
XLA Ops:
  12.5 4.4 collective-permute-start
  21.6 3.1 copy.127
  34.7 3.8 collective-permute-start.3
  90.8 11.2 %copy.151 = bf16[8,7,64,2,2,2,4,4,4]{2,1,8,7,6,5,4,3,0:T(8,128)(2,1)} copy(bf16[8,7,64,2,2,2,4,4,4]{2,0,8,7,6,5,4,3,1:T(8,128)(2,1)} %fusion.16) | data formatting | bytes 7340032 | tf_op jit(solution)/shard_map/stack | solution.py:148
  102.0 11.6 %reshape.747 = bf16[8,448,512]{1,2,0:T(8,128)(2,1)} reshape(bf16[8,7,64,2,2,2,4,4,4]{2,1,8,7,6,5,4,3,0:T(8,128)(2,1)} %copy.151) | data formatting | bytes 7340032 | tf_op jit(solution)/shard_map/reshape | solution.py:148
  113.6 4.6 multiply_convert_fusion.1
  123.7 6.5 %collective-permute-done.5 = bf16[16,8192]{1,0:T(8,128)(2,1)S(1)} collective-permute-done((bf16[16,8192]{1,0:T(8,128)(2,1)S(1)}, bf16[16,8192]{1,0:T(8,128)(2,1)S(1)}, u32[]{:S(2)}, u32[]{:S(2)}) %collective-permute-start.5) | collective-permute-done | bytes 262176 | tf_op jit(solution)/shard_map/ppermute | solution.py:14
  136.6 4.1 collective-permute-done.6
  148.8 3.7 convolution_bitcast_fusion.4
  152.5 4.1 convolution_bitcast_fusion
  156.6 8.8 %copy.155 = f32[8,448,512]{1,2,0:T(8,128)} copy(f32[8,448,512]{2,1,0:T(8,128)} %convolution_bitcast_fusion) | data formatting | bytes 14680064 | tf_op jit(solution)/shard_map/ok,bov->bkv/transpose | solution.py:271
  165.4 13.2 %reshape.754 = f32[8,7,64,2,2,2,4,4,4]{2,1,8,7,6,5,4,3,0:T(8,128)} reshape(f32[8,448,512]{1,2,0:T(8,128)} %copy.155) | data formatting | bytes 14680064 | tf_op jit(solution)/shard_map/reshape | solution.py:153
  178.6 53.0 %fusion.67 = (f32[8,1,64,2,2,2,4,4,4]{2,1,8,7,6,5,4,3,0:T(1,128)S(1)}, f32[8,1,64,2,2,2,4,4,4]{2,1,8,7,6,5,4,3,0:T(1,128)S(1)}, f32[8,1,64,2,2,2,4,4,4]{2,1,8,7,...) fusion(f32[8,7,64,2,2,2,4,4,4]{2,1,8,7,6,5,4,3,0:T(8,128)} %res, ...), kind=kLoop, calls=%fused_computation.173 | loop fusion | bytes 14680064 | tf_op jit(solution)/shard_map/slice | solution.py:159
  249.3 3.1 copy.166
  254.7 3.2 copy.170
  260.1 3.2 copy.162
  267.0 3.1 copy.174
  273.9 3.1 copy.178
  280.2 3.1 copy.182
  286.5 4.0 collective-permute-start.9
  313.6 6.5 %fusion = f32[8,64,2,2,2,4,4,4]{1,7,6,5,4,3,2,0:T(4,128)S(1)} fusion(f32[8,64,2,2,1,4,4,3]{1,7,6,5,4,3,2,0:T(4,128)} %slice.902, f32[8,64,2,2,1,4,4,3]{1,7,6,5,4,3,2,0:T(4,128)} %slice.900, f32[8,64,2,1,2,4,3,4]{1,7,6,5,4,3,2,0:T(4,128)} %slice.896, f32[8,64,2,1,2,4,3,4]{1,7,6,5,4,3,2,0:T(4,128)} %slice.894, f32[8,64,1,2,2,3,4,4]{1,7,6,5,4,3,2,0:T(4,128)} %slice.890, ...), kind=kLoop, calls=%fused_computation.16 | loop fusion | flops 6291456 | bytes 7602176 | tf_op jit(solution)/shard_map/add | solution.py:162
  322.3 6.4 %scatter-add.109 = f32[8,64,2,2,2,4,4,4]{1,7,6,5,4,3,2,0:T(4,128)S(1)} dynamic-update-slice(f32[8,64,2,2,2,4,4,4]{1,7,6,5,4,3,2,0:T(4,128)S(1)} %fusion.23, f32[8,64,2,2,1,4,4,1]{1,7,6,5,4,3,2,0:T(1,128)} %slice_add_fusion.5, s32[]{:T(128)} %constant.277.clone.1, s32[]{:T(128)} %constant.277.clone.1, s32[]{:T(128)} %constant.277.clone.1, s32[]{:T(128)} %constant.277.clone.1, s32[]{:T(128)} %constant.282.clone.1, ...) | dynamic-update-slice | bytes 262148 | tf_op jit(solution)/shard_map/scatter-add | solution.py:172
  331.8 6.4 %scatter-add.111 = f32[8,64,2,2,2,4,4,4]{1,7,6,5,4,3,2,0:T(4,128)S(1)} dynamic-update-slice(f32[8,64,2,2,2,4,4,4]{1,7,6,5,4,3,2,0:T(4,128)S(1)} %scatter-add.109, f32[8,64,2,2,1,4,4,1]{1,7,6,5,4,3,2,0:T(1,128)} %slice_add_fusion.4, s32[]{:T(128)} %constant.277.clone.1, s32[]{:T(128)} %constant.277.clone.1, s32[]{:T(128)} %constant.277.clone.1, s32[]{:T(128)} %constant.277.clone.1, ...) | dynamic-update-slice | bytes 262148 | tf_op jit(solution)/shard_map/scatter-add | solution.py:172
  361.8 237.7 %all-reduce.9.cloned.1.call-done = (f32[64,448]{1,0:T(8,128)}, f32[128,512]{1,0:T(8,128)}, f32[128,128]{0,1:T(8,128)}) async-done(((f32[64,448]{1,0:T(8,128)}, f32[128,512]{1,0:T(8,128)}, f32[128,128]{0,1:T(8,128)}), (f32[64,448]{1,0:T(8,128)}, f32[128,512]{1,0:T(8,128)}, f32[128,128]{0,1:T(8,128)})) %all-reduce.9.cloned.1.call-update) | async-done | bytes 442384 | tf_op jit(solution)/shard_map/psum | solution.py:281
  (295 shorter events, 183.4 us)
Async XLA Ops:
  7.2 111.6 %copy-start = (bf16[128,512]{1,0:T(8,128)(2,1)S(1)}, bf16[128,512]{1,0:T(8,128)(2,1)}, u32[]{:S(2)}) copy-start(bf16[128,512]{1,0:T(8,128)(2,1)} %param.32) | copy-start | bytes 393220
  7.2 592.3 %all-reduce.9.cloned.1.call-start = ((), (), s32[]{:S(2)}) async-start(), calls=%async_computation | async-start | bytes 917504 | tf_op jit(solution)/shard_map/psum | solution.py:281
  12.5 52.6 %collective-permute-start = (bf16[1,8,4096]{2,1,0:T(8,128)(2,1)}, bf16[1,8,4096]{2,1,0:T(8,128)(2,1)}, u32[]{:S(2)}, u32[]{:S(2)}) collective-permute-start(bf16[1,8,4096]{2,1,0:T(8,128)(2,1)} %copy.115), channel_id=1, source_target_pairs={{0,8},{8,16},{16,24},{24,32},{32,40},{40,48},{48,56},{56,64},{64,7... | collective-permute-start | bytes 196616 | tf_op jit(solution)/shard_map/ppermute | solution.py:22
  19.6 45.6 %collective-permute-start.1 = (bf16[1,8,4096]{2,1,0:T(8,128)(2,1)}, bf16[1,8,4096]{2,1,0:T(8,128)(2,1)}, u32[]{:S(2)}, u32[]{:S(2)}) collective-permute-start(bf16[1,8,4096]{2,1,0:T(8,128)(2,1)} %copy.122), channel_id=1, source_target_pairs={{8,0},{16,8},{24,16},{32,24},{40,32},{48,40},{56,48},{64,56},{72,6... | collective-permute-start | bytes 196616 | tf_op jit(solution)/shard_map/ppermute | solution.py:25
  26.8 38.3 %collective-permute-start.2 = (bf16[1,8,4096]{2,1,0:T(8,128)(2,1)}, bf16[1,8,4096]{2,1,0:T(8,128)(2,1)}, u32[]{:S(2)}, u32[]{:S(2)}) collective-permute-start(bf16[1,8,4096]{2,1,0:T(8,128)(2,1)} %copy.129), channel_id=1, source_target_pairs={{0,1},{1,2},{2,3},{3,4},{4,5},{5,6},{6,7},{8,9},{9,10},{10,11},{11... | collective-permute-start | bytes 196616 | tf_op jit(solution)/shard_map/ppermute | solution.py:22
  34.7 30.5 %collective-permute-start.3 = (bf16[1,8,4096]{2,1,0:T(8,128)(2,1)}, bf16[1,8,4096]{2,1,0:T(8,128)(2,1)}, u32[]{:S(2)}, u32[]{:S(2)}) collective-permute-start(bf16[1,8,4096]{2,1,0:T(8,128)(2,1)} %copy.136), channel_id=1, source_target_pairs={{1,0},{2,1},{3,2},{4,3},{5,4},{6,5},{7,6},{9,8},{10,9},{11,10},{12... | collective-permute-start | bytes 196616 | tf_op jit(solution)/shard_map/ppermute | solution.py:25
  77.0 6.0 copy-start.8
  77.0 6.0 copy-start.14
  102.0 11.6 %copy-start.28 = (bf16[64,448]{1,0:T(8,128)(2,1)S(1)}, bf16[64,448]{1,0:T(8,128)(2,1)}, u32[]{:S(2)}) copy-start(bf16[64,448]{1,0:T(8,128)(2,1)} %param.31) | copy-start | bytes 172036
  118.8 12.2 %copy-start.27 = (bf16[1,512,128]{2,1,0:T(8,128)(2,1)S(1)}, bf16[1,512,128]{2,1,0:T(8,128)(2,1)}, u32[]{:S(2)}) copy-start(bf16[1,512,128]{2,1,0:T(8,128)(2,1)} %param.35) | copy-start | bytes 393220
  118.8 12.2 %copy-start.40 = (bf16[128,128]{1,0:T(8,128)(2,1)S(1)}, bf16[128,128]{1,0:T(8,128)(2,1)}, u32[]{:S(2)}) copy-start(bf16[128,128]{1,0:T(8,128)(2,1)} %param.33) | copy-start | bytes 98308
  119.4 1.4 collective-permute-start.4
  120.8 9.4 %collective-permute-start.5 = (bf16[16,8192]{1,0:T(8,128)(2,1)S(1)}, bf16[16,8192]{1,0:T(8,128)(2,1)S(1)}, u32[]{:S(2)}, u32[]{:S(2)}) collective-permute-start(bf16[16,8192]{1,0:T(8,128)(2,1)S(1)} %pad_maximum_fusion), channel_id=1, source_target_pairs={{0,8},{8,0},{16,24},{24,16},{32,40},{40,32},{48,56},{56,48},{64,72... | collective-permute-start | bytes 786440 | tf_op jit(solution)/shard_map/ppermute | solution.py:14
  132.7 8.3 %copy-start.41 = (bf16[128,128]{1,0:T(8,128)(2,1)S(1)}, bf16[128,128]{1,0:T(8,128)(2,1)}, u32[]{:S(2)}) copy-start(bf16[128,128]{1,0:T(8,128)(2,1)} %param.33) | copy-start | bytes 98308
  132.7 8.0 %collective-permute-start.6 = (bf16[16,8192]{1,0:T(8,128)(2,1)S(1)}, bf16[16,8192]{1,0:T(8,128)(2,1)S(1)}, u32[]{:S(2)}, u32[]{:S(2)}) collective-permute-start(bf16[16,8192]{1,0:T(8,128)(2,1)S(1)} %pad_maximum_fusion.1), channel_id=1, source_target_pairs={{0,8},{8,0},{16,24},{24,16},{32,40},{40,32},{48,56},{56,48},{64,72... | collective-permute-start | bytes 786440 | tf_op jit(solution)/shard_map/ppermute | solution.py:14
  140.8 1.4 collective-permute-start.7
  286.5 66.8 %collective-permute-start.9 = (bf16[1,8,4096]{2,1,0:T(8,128)(2,1)}, bf16[1,8,4096]{2,1,0:T(8,128)(2,1)}, u32[]{:S(2)}, u32[]{:S(2)}) collective-permute-start(bf16[1,8,4096]{2,1,0:T(8,128)(2,1)} %fusion.53), channel_id=1, source_target_pairs={{0,8},{8,16},{16,24},{24,32},{32,40},{40,48},{48,56},{56,64},{64,7... | collective-permute-start | bytes 196616 | tf_op jit(solution)/shard_map/ppermute | solution.py:22
  290.5 57.6 %collective-permute-start.10 = (bf16[1,8,4096]{2,1,0:T(8,128)(2,1)}, bf16[1,8,4096]{2,1,0:T(8,128)(2,1)}, u32[]{:S(2)}, u32[]{:S(2)}) collective-permute-start(bf16[1,8,4096]{2,1,0:T(8,128)(2,1)} %fusion.54), channel_id=1, source_target_pairs={{1,0},{2,1},{3,2},{4,3},{5,4},{6,5},{7,6},{9,8},{10,9},{11,10},{12... | collective-permute-start | bytes 196616 | tf_op jit(solution)/shard_map/ppermute | solution.py:25
  292.4 50.8 %collective-permute-start.8 = (bf16[1,8,4096]{2,1,0:T(8,128)(2,1)}, bf16[1,8,4096]{2,1,0:T(8,128)(2,1)}, u32[]{:S(2)}, u32[]{:S(2)}) collective-permute-start(bf16[1,8,4096]{2,1,0:T(8,128)(2,1)} %fusion.52), channel_id=1, source_target_pairs={{8,0},{16,8},{24,16},{32,24},{40,32},{48,40},{56,48},{64,56},{72,6... | collective-permute-start | bytes 196616 | tf_op jit(solution)/shard_map/ppermute | solution.py:25
  293.7 44.5 %collective-permute-start.11 = (bf16[1,8,4096]{2,1,0:T(8,128)(2,1)}, bf16[1,8,4096]{2,1,0:T(8,128)(2,1)}, u32[]{:S(2)}, u32[]{:S(2)}) collective-permute-start(bf16[1,8,4096]{2,1,0:T(8,128)(2,1)} %fusion.55), channel_id=1, source_target_pairs={{0,1},{1,2},{2,3},{3,4},{4,5},{5,6},{6,7},{8,9},{9,10},{10,11},{11... | collective-permute-start | bytes 196616 | tf_op jit(solution)/shard_map/ppermute | solution.py:22
  313.6 6.5 %copy-start.17 = (f32[8,64,1,2,2,1,4,4]{1,7,6,5,4,3,2,0:T(4,128)S(1)}, f32[8,64,1,2,2,1,4,4]{1,7,6,5,4,3,2,0:T(4,128)}, u32[]{:S(2)}) copy-start(f32[8,64,1,2,2,1,4,4]{1,7,6,5,4,3,2,0:T(4,128)} %copy.165) | copy-start | bytes 393220
  313.6 6.7 %copy-start.19 = (f32[8,64,1,2,2,1,4,4]{1,7,6,5,4,3,2,0:T(4,128)S(1)}, f32[8,64,1,2,2,1,4,4]{1,7,6,5,4,3,2,0:T(4,128)}, u32[]{:S(2)}) copy-start(f32[8,64,1,2,2,1,4,4]{1,7,6,5,4,3,2,0:T(4,128)} %copy.169) | copy-start | bytes 393220
  313.6 6.8 %copy-start.16 = (f32[8,64,2,1,2,4,1,4]{1,7,6,5,4,3,2,0:T(4,128)S(1)}, f32[8,64,2,1,2,4,1,4]{1,7,6,5,4,3,2,0:T(4,128)}, u32[]{:S(2)}) copy-start(f32[8,64,2,1,2,4,1,4]{1,7,6,5,4,3,2,0:T(4,128)} %copy.173) | copy-start | bytes 393220
  358.7 245.6 %copy-start.1 = (bf16[128,512]{1,0:T(8,128)(2,1)S(1)}, bf16[128,512]{1,0:T(8,128)(2,1)}, u32[]{:S(2)}) copy-start(bf16[128,512]{1,0:T(8,128)(2,1)} %param.32) | copy-start | bytes 393220
  (33 other events, 79.7 us)
Sparse Core Ops, SparseCore 0:
  338.3 261.1 all-reduce.8
where the time goes:
time: 619 us; the launch traced here: 612 us
  local copies, waits for them, and re-layouts  264 us (43%)
  waiting for transfers between devices  250 us (40%)
  other arithmetic  37.3 us (6%)
  starting transfers between devices  26.2 us (4%)
  matrix products  18.1 us (3%)
  between operations  16.2 us (3%)
    psum x1, waiting for transfers between devices, body(): summed = lax.psum((conv_part, down_part, head_part), ('gx', 'gy'))  238 us
    slice x1, local copies, waits for them, and re-layouts, stack_grad(): moved, plane = minus_back(parts[:, direction + 1], axis_number)  53 us
    convert_element_type x8, local copies, waits for them, and re-layouts, planes(): return rows.astype(jnp.float32).reshape(number, channels, 2, 2, 4, 4)  20 us
    slice x12, local copies, waits for them, and re-layouts, face_of(): lax.index_in_dim(plane, 1 if upper else 0, 2 + axis_number, keepdims=False)  16.3 us
    reshape x1, local copies, waits for them, and re-layouts, stack_grad(): parts = taps_grad.reshape(number, 7, channels, 2, 2, 2, 4, 4, 4)  13.2 us
    ppermute x4, starting transfers between devices, padded(): lax.ppermute(lax.slice_in_dim(block, block.shape[dim] - width, None, axis...  12.9 us
    scatter-add x2, local copies, waits for them, and re-layouts, stack_grad(): grad_cube.at[face_index(direction // 2, direction % 2 == 0)].add(shaped)  12.7 us
    ppermute x4, waiting for transfers between devices, from_partner(): return lax.ppermute(block, axis, route)  12.4 us
  transfers between devices with their start and end apart: 13, of which 5 were waited for; matrix products, arithmetic and copies ran while one was open for 18% of the time, Pallas kernels for 0%

commit v1 on v0

--- a/solution.py
+++ b/solution.py
@@ -278,7 +278,7 @@
         number, channels, 512
     )
     features_grad = jnp.where(active[:, None, None], total_grad, 0.0).astype(jnp.bfloat16)
-    summed = lax.psum((conv_part, down_part, head_part), ("gx", "gy"))
+    summed = lax.psum(lax.psum((conv_part, down_part, head_part), "gy"), "gx")
     scale = float(number * lax.axis_size("gx") * lax.axis_size("gy")) ** (-0.5)
     return (latent, features_grad, summed[0] * scale, summed[1] * scale, summed[2] * scale)
 

time: 619 us -> 582 us (0.940)
  waiting for transfers between devices: 250 us -> 213 us
    psum x1 -> x2, waiting for transfers between devices: 238 us -> 200 us  [body(): summed = lax.psum(lax.psum((conv_part, down_part, head_part), 'gy'), 'gx')]
  transfers between devices with their start and end apart: 13 -> 14, of which waited for: 5 -> 6; matrix products, arithmetic and copies ran while one was open for 18% -> 19% of each run, Pallas kernels for 0% -> 0%
where the time goes in v1:
time: 582 us; the launch traced here: 575 us
  local copies, waits for them, and re-layouts  264 us (45%)
  waiting for transfers between devices  213 us (37%)
  other arithmetic  37.6 us (6%)
  starting transfers between devices  26.3 us (5%)
  matrix products  18.1 us (3%)
  between operations  16.2 us (3%)
    psum x2, waiting for transfers between devices, body(): summed = lax.psum(lax.psum((conv_part, down_part, head_part), 'gy'), 'gx')  200 us
    slice x1, local copies, waits for them, and re-layouts, stack_grad(): moved, plane = minus_back(parts[:, direction + 1], axis_number)  53.6 us
    convert_element_type x8, local copies, waits for them, and re-layouts, planes(): return rows.astype(jnp.float32).reshape(number, channels, 2, 2, 4, 4)  19.8 us
    slice x12, local copies, waits for them, and re-layouts, face_of(): lax.index_in_dim(plane, 1 if upper else 0, 2 + axis_number, keepdims=False)  16.3 us
    reshape x1, local copies, waits for them, and re-layouts, stack_grad(): parts = taps_grad.reshape(number, 7, channels, 2, 2, 2, 4, 4, 4)  13.2 us
    ppermute x4, starting transfers between devices, padded(): lax.ppermute(lax.slice_in_dim(block, block.shape[dim] - width, None, axis...  12.7 us
    scatter-add x2, local copies, waits for them, and re-layouts, stack_grad(): grad_cube.at[face_index(direction // 2, direction % 2 == 0)].add(shaped)  12.7 us
    ppermute x4, waiting for transfers between devices, from_partner(): return lax.ppermute(block, axis, route)  12.4 us
  transfers between devices with their start and end apart: 14, of which 6 were waited for; matrix products, arithmetic and copies ran while one was open for 19% of the time, Pallas kernels for 0%

profile of v1, /device:TPU:2, one launch (start us, length us, event | category | flops | bytes accessed | tf_op | source)
XLA Modules:
  0.0 575.1 jit_solution(17583101282323807913)
XLA Ops:
  12.6 4.5 collective-permute-start
  34.8 3.8 collective-permute-start.3
  90.9 11.2 %copy.151 = bf16[8,7,64,2,2,2,4,4,4]{2,1,8,7,6,5,4,3,0:T(8,128)(2,1)} copy(bf16[8,7,64,2,2,2,4,4,4]{2,0,8,7,6,5,4,3,1:T(8,128)(2,1)} %fusion.16) | data formatting | bytes 7340032 | tf_op jit(solution)/shard_map/stack | solution.py:148
  102.2 11.6 %reshape.747 = bf16[8,448,512]{1,2,0:T(8,128)(2,1)} reshape(bf16[8,7,64,2,2,2,4,4,4]{2,1,8,7,6,5,4,3,0:T(8,128)(2,1)} %copy.151) | data formatting | bytes 7340032 | tf_op jit(solution)/shard_map/reshape | solution.py:148
  113.8 4.6 multiply_convert_fusion.1
  123.8 6.5 %collective-permute-done.5 = bf16[16,8192]{1,0:T(8,128)(2,1)S(1)} collective-permute-done((bf16[16,8192]{1,0:T(8,128)(2,1)S(1)}, bf16[16,8192]{1,0:T(8,128)(2,1)S(1)}, u32[]{:S(2)}, u32[]{:S(2)}) %collective-permute-start.5) | collective-permute-done | bytes 262176 | tf_op jit(solution)/shard_map/ppermute | solution.py:14
  136.8 4.1 collective-permute-done.6
  148.9 3.7 convolution_bitcast_fusion.4
  152.7 4.1 convolution_bitcast_fusion
  156.7 8.8 %copy.155 = f32[8,448,512]{1,2,0:T(8,128)} copy(f32[8,448,512]{2,1,0:T(8,128)} %convolution_bitcast_fusion) | data formatting | bytes 14680064 | tf_op jit(solution)/shard_map/ok,bov->bkv/transpose | solution.py:271
  165.6 13.2 %reshape.754 = f32[8,7,64,2,2,2,4,4,4]{2,1,8,7,6,5,4,3,0:T(8,128)} reshape(f32[8,448,512]{1,2,0:T(8,128)} %copy.155) | data formatting | bytes 14680064 | tf_op jit(solution)/shard_map/reshape | solution.py:153
  178.7 53.6 %fusion.67 = (f32[8,1,64,2,2,2,4,4,4]{2,1,8,7,6,5,4,3,0:T(1,128)S(1)}, f32[8,1,64,2,2,2,4,4,4]{2,1,8,7,6,5,4,3,0:T(1,128)S(1)}, f32[8,1,64,2,2,2,4,4,4]{2,1,8,7,...) fusion(f32[8,7,64,2,2,2,4,4,4]{2,1,8,7,6,5,4,3,0:T(8,128)} %res, ...), kind=kLoop, calls=%fused_computation.173 | loop fusion | bytes 14680064 | tf_op jit(solution)/shard_map/slice | solution.py:159
  250.2 3.1 copy.166
  255.5 3.2 copy.170
  261.1 3.2 copy.162
  268.0 3.1 copy.174
  275.0 3.1 copy.178
  281.2 3.1 copy.182
  287.5 4.0 collective-permute-start.9
  314.3 6.5 %fusion = f32[8,64,2,2,2,4,4,4]{1,7,6,5,4,3,2,0:T(4,128)S(1)} fusion(f32[8,64,2,2,1,4,4,3]{1,7,6,5,4,3,2,0:T(4,128)} %slice.902, f32[8,64,2,2,1,4,4,3]{1,7,6,5,4,3,2,0:T(4,128)} %slice.900, f32[8,64,2,1,2,4,3,4]{1,7,6,5,4,3,2,0:T(4,128)} %slice.896, f32[8,64,2,1,2,4,3,4]{1,7,6,5,4,3,2,0:T(4,128)} %slice.894, f32[8,64,1,2,2,3,4,4]{1,7,6,5,4,3,2,0:T(4,128)} %slice.890, ...), kind=kLoop, calls=%fused_computation.16 | loop fusion | flops 6291456 | bytes 7602176 | tf_op jit(solution)/shard_map/add | solution.py:162
  323.1 6.4 %scatter-add.109 = f32[8,64,2,2,2,4,4,4]{1,7,6,5,4,3,2,0:T(4,128)S(1)} dynamic-update-slice(f32[8,64,2,2,2,4,4,4]{1,7,6,5,4,3,2,0:T(4,128)S(1)} %fusion.23, f32[8,64,2,2,1,4,4,1]{1,7,6,5,4,3,2,0:T(1,128)} %slice_add_fusion.5, s32[]{:T(128)} %constant.277.clone.1, s32[]{:T(128)} %constant.277.clone.1, s32[]{:T(128)} %constant.277.clone.1, s32[]{:T(128)} %constant.277.clone.1, s32[]{:T(128)} %constant.282.clone.1, ...) | dynamic-update-slice | bytes 262148 | tf_op jit(solution)/shard_map/scatter-add | solution.py:172
  332.6 6.4 %scatter-add.111 = f32[8,64,2,2,2,4,4,4]{1,7,6,5,4,3,2,0:T(4,128)S(1)} dynamic-update-slice(f32[8,64,2,2,2,4,4,4]{1,7,6,5,4,3,2,0:T(4,128)S(1)} %scatter-add.109, f32[8,64,2,2,1,4,4,1]{1,7,6,5,4,3,2,0:T(1,128)} %slice_add_fusion.4, s32[]{:T(128)} %constant.277.clone.1, s32[]{:T(128)} %constant.277.clone.1, s32[]{:T(128)} %constant.277.clone.1, s32[]{:T(128)} %constant.277.clone.1, ...) | dynamic-update-slice | bytes 262148 | tf_op jit(solution)/shard_map/scatter-add | solution.py:172
  359.5 49.2 %all-reduce.13.cloned.1.call-done = (f32[64,448]{1,0:T(8,128)}, f32[128,512]{1,0:T(8,128)}, f32[128,128]{0,1:T(8,128)}) async-done(((f32[64,448]{1,0:T(8,128)}, f32[128,512]{1,0:T(8,128)}, f32[128,128]{0,1:T(8,128)}), (f32[64,448]{1,0:T(8,128)}, f32[128,512]{1,0:T(8,128)}, f32[128,128]{0,1:T(8,128)})) %all-reduce.13.cloned.1.call-update) | async-done | bytes 442384 | tf_op jit(solution)/shard_map/psum | solution.py:281
  412.0 151.0 %all-reduce.11.cloned.1.call-done = (f32[64,448]{1,0:T(8,128)}, f32[128,512]{1,0:T(8,128)}, f32[128,128]{0,1:T(8,128)}) async-done(((f32[64,448]{1,0:T(8,128)}, f32[128,512]{1,0:T(8,128)}, f32[128,128]{0,1:T(8,128)}), (f32[64,448]{1,0:T(8,128)}, f32[128,512]{1,0:T(8,128)}, f32[128,128]{0,1:T(8,128)})) %all-reduce.11.cloned.1.call-update) | async-done | bytes 442384 | tf_op jit(solution)/shard_map/psum | solution.py:281
  (298 shorter events, 186.8 us)
Async XLA Ops:
  7.2 111.7 %copy-start = (bf16[128,512]{1,0:T(8,128)(2,1)S(1)}, bf16[128,512]{1,0:T(8,128)(2,1)}, u32[]{:S(2)}) copy-start(bf16[128,512]{1,0:T(8,128)(2,1)} %param.32) | copy-start | bytes 393220
  7.2 401.5 %all-reduce.13.cloned.1.call-start = ((), (), s32[]{:S(2)}) async-start(), calls=%async_computation.1 | async-start | bytes 917504 | tf_op jit(solution)/shard_map/psum | solution.py:281
  12.6 52.8 %collective-permute-start = (bf16[1,8,4096]{2,1,0:T(8,128)(2,1)}, bf16[1,8,4096]{2,1,0:T(8,128)(2,1)}, u32[]{:S(2)}, u32[]{:S(2)}) collective-permute-start(bf16[1,8,4096]{2,1,0:T(8,128)(2,1)} %copy.115), channel_id=1, source_target_pairs={{0,8},{8,16},{16,24},{24,32},{32,40},{40,48},{48,56},{56,64},{64,7... | collective-permute-start | bytes 196616 | tf_op jit(solution)/shard_map/ppermute | solution.py:22
  19.6 45.8 %collective-permute-start.1 = (bf16[1,8,4096]{2,1,0:T(8,128)(2,1)}, bf16[1,8,4096]{2,1,0:T(8,128)(2,1)}, u32[]{:S(2)}, u32[]{:S(2)}) collective-permute-start(bf16[1,8,4096]{2,1,0:T(8,128)(2,1)} %copy.122), channel_id=1, source_target_pairs={{8,0},{16,8},{24,16},{32,24},{40,32},{48,40},{56,48},{64,56},{72,6... | collective-permute-start | bytes 196616 | tf_op jit(solution)/shard_map/ppermute | solution.py:25
  26.9 38.5 %collective-permute-start.2 = (bf16[1,8,4096]{2,1,0:T(8,128)(2,1)}, bf16[1,8,4096]{2,1,0:T(8,128)(2,1)}, u32[]{:S(2)}, u32[]{:S(2)}) collective-permute-start(bf16[1,8,4096]{2,1,0:T(8,128)(2,1)} %copy.129), channel_id=1, source_target_pairs={{0,1},{1,2},{2,3},{3,4},{4,5},{5,6},{6,7},{8,9},{9,10},{10,11},{11... | collective-permute-start | bytes 196616 | tf_op jit(solution)/shard_map/ppermute | solution.py:22
  34.8 30.6 %collective-permute-start.3 = (bf16[1,8,4096]{2,1,0:T(8,128)(2,1)}, bf16[1,8,4096]{2,1,0:T(8,128)(2,1)}, u32[]{:S(2)}, u32[]{:S(2)}) collective-permute-start(bf16[1,8,4096]{2,1,0:T(8,128)(2,1)} %copy.136), channel_id=1, source_target_pairs={{1,0},{2,1},{3,2},{4,3},{5,4},{6,5},{7,6},{9,8},{10,9},{11,10},{12... | collective-permute-start | bytes 196616 | tf_op jit(solution)/shard_map/ppermute | solution.py:25
  77.2 5.9 %copy-start.8 = (bf16[8,64,1,2,2,4,4,4]{1,0,7,6,5,4,3,2:T(8,128)(2,1)S(1)}, bf16[8,64,1,2,2,4,4,4]{1,0,7,6,5,4,3,2:T(8,128)(2,1)}, u32[]{:S(2)}) copy-start(bf16[8,64,1,2,2,4,4,4]{1,0,7,6,5,4,3,2:T(8,128)(2,1)} %get-tuple-element.166) | copy-start | bytes 786436
  102.2 11.6 %copy-start.28 = (bf16[64,448]{1,0:T(8,128)(2,1)S(1)}, bf16[64,448]{1,0:T(8,128)(2,1)}, u32[]{:S(2)}) copy-start(bf16[64,448]{1,0:T(8,128)(2,1)} %param.31) | copy-start | bytes 172036
  118.9 12.2 %copy-start.27 = (bf16[1,512,128]{2,1,0:T(8,128)(2,1)S(1)}, bf16[1,512,128]{2,1,0:T(8,128)(2,1)}, u32[]{:S(2)}) copy-start(bf16[1,512,128]{2,1,0:T(8,128)(2,1)} %param.35) | copy-start | bytes 393220
  118.9 12.2 %copy-start.40 = (bf16[128,128]{1,0:T(8,128)(2,1)S(1)}, bf16[128,128]{1,0:T(8,128)(2,1)}, u32[]{:S(2)}) copy-start(bf16[128,128]{1,0:T(8,128)(2,1)} %param.33) | copy-start | bytes 98308
  119.5 1.4 collective-permute-start.4
  121.0 9.4 %collective-permute-start.5 = (bf16[16,8192]{1,0:T(8,128)(2,1)S(1)}, bf16[16,8192]{1,0:T(8,128)(2,1)S(1)}, u32[]{:S(2)}, u32[]{:S(2)}) collective-permute-start(bf16[16,8192]{1,0:T(8,128)(2,1)S(1)} %pad_maximum_fusion), channel_id=1, source_target_pairs={{0,8},{8,0},{16,24},{24,16},{32,40},{40,32},{48,56},{56,48},{64,72... | collective-permute-start | bytes 786440 | tf_op jit(solution)/shard_map/ppermute | solution.py:14
  132.8 8.2 %copy-start.41 = (bf16[128,128]{1,0:T(8,128)(2,1)S(1)}, bf16[128,128]{1,0:T(8,128)(2,1)}, u32[]{:S(2)}) copy-start(bf16[128,128]{1,0:T(8,128)(2,1)} %param.33) | copy-start | bytes 98308
  132.9 8.0 %collective-permute-start.6 = (bf16[16,8192]{1,0:T(8,128)(2,1)S(1)}, bf16[16,8192]{1,0:T(8,128)(2,1)S(1)}, u32[]{:S(2)}, u32[]{:S(2)}) collective-permute-start(bf16[16,8192]{1,0:T(8,128)(2,1)S(1)} %pad_maximum_fusion.1), channel_id=1, source_target_pairs={{0,8},{8,0},{16,24},{24,16},{32,40},{40,32},{48,56},{56,48},{64,72... | collective-permute-start | bytes 786440 | tf_op jit(solution)/shard_map/ppermute | solution.py:14
  141.0 1.4 collective-permute-start.7
  287.5 66.6 %collective-permute-start.9 = (bf16[1,8,4096]{2,1,0:T(8,128)(2,1)}, bf16[1,8,4096]{2,1,0:T(8,128)(2,1)}, u32[]{:S(2)}, u32[]{:S(2)}) collective-permute-start(bf16[1,8,4096]{2,1,0:T(8,128)(2,1)} %fusion.53), channel_id=1, source_target_pairs={{0,8},{8,16},{16,24},{24,32},{32,40},{40,48},{48,56},{56,64},{64,7... | collective-permute-start | bytes 196616 | tf_op jit(solution)/shard_map/ppermute | solution.py:22
  291.5 57.7 %collective-permute-start.10 = (bf16[1,8,4096]{2,1,0:T(8,128)(2,1)}, bf16[1,8,4096]{2,1,0:T(8,128)(2,1)}, u32[]{:S(2)}, u32[]{:S(2)}) collective-permute-start(bf16[1,8,4096]{2,1,0:T(8,128)(2,1)} %fusion.54), channel_id=1, source_target_pairs={{1,0},{2,1},{3,2},{4,3},{5,4},{6,5},{7,6},{9,8},{10,9},{11,10},{12... | collective-permute-start | bytes 196616 | tf_op jit(solution)/shard_map/ppermute | solution.py:25
  293.4 50.8 %collective-permute-start.8 = (bf16[1,8,4096]{2,1,0:T(8,128)(2,1)}, bf16[1,8,4096]{2,1,0:T(8,128)(2,1)}, u32[]{:S(2)}, u32[]{:S(2)}) collective-permute-start(bf16[1,8,4096]{2,1,0:T(8,128)(2,1)} %fusion.52), channel_id=1, source_target_pairs={{8,0},{16,8},{24,16},{32,24},{40,32},{48,40},{56,48},{64,56},{72,6... | collective-permute-start | bytes 196616 | tf_op jit(solution)/shard_map/ppermute | solution.py:25
  294.7 44.6 %collective-permute-start.11 = (bf16[1,8,4096]{2,1,0:T(8,128)(2,1)}, bf16[1,8,4096]{2,1,0:T(8,128)(2,1)}, u32[]{:S(2)}, u32[]{:S(2)}) collective-permute-start(bf16[1,8,4096]{2,1,0:T(8,128)(2,1)} %fusion.55), channel_id=1, source_target_pairs={{0,1},{1,2},{2,3},{3,4},{4,5},{5,6},{6,7},{8,9},{9,10},{10,11},{11... | collective-permute-start | bytes 196616 | tf_op jit(solution)/shard_map/ppermute | solution.py:22
  314.3 6.5 %copy-start.17 = (f32[8,64,1,2,2,1,4,4]{1,7,6,5,4,3,2,0:T(4,128)S(1)}, f32[8,64,1,2,2,1,4,4]{1,7,6,5,4,3,2,0:T(4,128)}, u32[]{:S(2)}) copy-start(f32[8,64,1,2,2,1,4,4]{1,7,6,5,4,3,2,0:T(4,128)} %copy.165) | copy-start | bytes 393220
  314.3 6.7 %copy-start.19 = (f32[8,64,1,2,2,1,4,4]{1,7,6,5,4,3,2,0:T(4,128)S(1)}, f32[8,64,1,2,2,1,4,4]{1,7,6,5,4,3,2,0:T(4,128)}, u32[]{:S(2)}) copy-start(f32[8,64,1,2,2,1,4,4]{1,7,6,5,4,3,2,0:T(4,128)} %copy.169) | copy-start | bytes 393220
  314.3 6.8 %copy-start.16 = (f32[8,64,2,1,2,4,1,4]{1,7,6,5,4,3,2,0:T(4,128)S(1)}, f32[8,64,2,1,2,4,1,4]{1,7,6,5,4,3,2,0:T(4,128)}, u32[]{:S(2)}) copy-start(f32[8,64,2,1,2,4,1,4]{1,7,6,5,4,3,2,0:T(4,128)} %copy.173) | copy-start | bytes 393220
  339.0 224.0 %all-reduce.11.cloned.1.call-start = ((), (), s32[]{:S(2)}) async-start(), calls=%async_computation | async-start | bytes 917504 | tf_op jit(solution)/shard_map/psum | solution.py:281
  408.8 159.0 %copy-start.1 = (bf16[128,512]{1,0:T(8,128)(2,1)S(1)}, bf16[128,512]{1,0:T(8,128)(2,1)}, u32[]{:S(2)}) copy-start(bf16[128,512]{1,0:T(8,128)(2,1)} %param.32) | copy-start | bytes 393220
  (34 other events, 85.5 us)
Sparse Core Ops, SparseCore 0:
  339.1 69.5 all-reduce.12
  412.4 150.5 all-reduce.10
